TPU v7x, 32 devices: a whole 2x2x4 slice. The times are simulated.
32 devices in a mesh: chan: 8 (over z, y), tm: 4 (over x, core).
Axes of the slice: x: 2, y: 2, z: 4, core: 2. Of those that a mesh axis runs over, the one named last changes fastest.
Arguments:
- samples: float32 [256, 4096], P('chan', 'tm'), may hold values from -6 to 6
- thresholds: int32 [3, 6], replicated, may hold values from 8 to 48
- sources: int32 [64], replicated, may hold values from 0 to 255
Outputs:
- correlations: float32 [64, 256, 512], P(None, ('chan', 'tm'))
Inputs may be any that keep to these rules, and one draw needn't show every extreme that they name: Channel numbers of the virtual sources; two may be equal.
All inputs are finite; a program needn't handle non-finite values.
Results may differ from a plain program's by a relative error of at most 0.0074.
Values may be sent and summed in bfloat16 or wider, within the bound.
A program may use at most 64 MiB of HBM per device.

v0:
```python
import math

import jax
import jax.numpy as jnp
import numpy as np
from jax import lax
from jax.experimental import pallas as pl
from jax.experimental.pallas import tpu as pltpu
from jax.sharding import PartitionSpec as P

N = 1024
LEVELS = 3
BINS = 512
LAGS = 512
BLOCK = 128
HALF = 64
MESH = pl.DeviceIdType.MESH

daubechies = [
    0.2303778133088964,
    0.7148465705529155,
    0.6308807679298587,
    -0.0279837694168599,
    -0.1870348117190931,
    0.0308413818355607,
    0.0328830116668852,
    -0.010597401785069,
]


def filter_bank():
    lowpass = list(daubechies)
    highpass = [(1.0 if k % 2 == 0 else -1.0) * daubechies[7 - k] for k in range(8)]
    return [(lowpass, highpass), (lowpass[::-1], highpass[::-1])]


def bank_matrix(length):
    half = length // 2
    out = np.zeros((2, 2, half, length))
    rows = np.arange(half)
    for tree, pair in enumerate(filter_bank()):
        for band, taps in enumerate(pair):
            for k in range(8):
                np.add.at(out[tree, band], (rows, (2 * rows + k - 3) % length), taps[k])
    return out.reshape(2, length, length)


def halves(matrix):
    m32 = np.asarray(matrix, np.float32)
    hi = m32.astype(jnp.bfloat16)
    lo = (m32 - hi.astype(np.float32)).astype(jnp.bfloat16)
    return np.stack([hi, lo])


def dft_table():
    t = np.arange(N)
    f = np.arange(BINS)
    phases = ((t[:, None] * f[None, :]) % N).astype(np.float64) * (2.0 * math.pi / N)
    table = np.concatenate([np.cos(phases), -np.sin(phases)], 1)
    return table.astype(np.float32).astype(jnp.bfloat16)


def split(x):
    hi = x.astype(jnp.bfloat16)
    lo = (x - hi.astype(jnp.float32)).astype(jnp.bfloat16)
    return hi, lo


def dot(a, b, trans_b):
    dims = (((1,), (1 if trans_b else 0,)), ((), ()))
    return lax.dot_general(a, b, dims, preferred_element_type=jnp.float32)


def dot3(a, b, trans_b=False):
    return dot(a[0], b[0], trans_b) + (dot(a[1], b[0], trans_b) + dot(a[0], b[1], trans_b))


def greet_all():
    n_tm = lax.axis_size("tm")
    n = lax.axis_size("chan") * n_tm
    me = lax.axis_index("chan") * n_tm + lax.axis_index("tm")
    barrier = pltpu.get_barrier_semaphore()

    def greet(k, carry):
        d = lax.rem(me + k, n)
        pl.semaphore_signal(
            barrier, inc=1, device_id=(d // n_tm, lax.rem(d, n_tm)), device_id_type=MESH
        )
        return carry

    lax.fori_loop(1, n, greet, 0)
    pl.semaphore_wait(barrier, n - 1)


def gather_kernel(samples, slab, blocks, edge, send, recv, edge_send, edge_recv, own):
    n_chan, n_tm = lax.axis_size("chan"), lax.axis_size("tm")
    c, t = lax.axis_index("chan"), lax.axis_index("tm")
    rows, width = samples.shape
    count = width // BLOCK
    rep = n_chan // count
    values = samples[...]
    first = jnp.concatenate([values[:, width - HALF :], values[:, :HALF]], 1)
    blocks[0] = first
    blocks[count] = first
    for j in range(1, count):
        blocks[j] = values[:, BLOCK * j - HALF : BLOCK * j + HALF]
    greet_all()
    mine = pl.ds(pl.multiple_of(c * rows, rows), rows)
    place = c // rep

    def remote(to):
        return pltpu.make_async_remote_copy(
            src_ref=blocks.at[pl.ds(to // rep, 2)],
            dst_ref=slab.at[:, mine, :],
            send_sem=send.at[to],
            recv_sem=recv.at[c],
            device_id=(to, t),
            device_id_type=MESH,
        )

    def incoming(source):
        return pltpu.make_async_remote_copy(
            src_ref=blocks.at[pl.ds(0, 2)],
            dst_ref=slab.at[:, pl.ds(pl.multiple_of(source * rows, rows), rows), :],
            send_sem=send.at[source],
            recv_sem=recv.at[source],
            device_id=(source, t),
            device_id_type=MESH,
        )

    def rim(to, shift, r):
        return pltpu.make_async_remote_copy(
            src_ref=blocks.at[0],
            dst_ref=edge.at[mine, :],
            send_sem=edge_send.at[r],
            recv_sem=edge_recv.at[c],
            device_id=(to, lax.rem(t + shift, n_tm)),
            device_id_type=MESH,
        )

    for r in range(rep):
        rim(r, 1, r).start()
        rim((count - 1) * rep + r, n_tm - 1, rep + r).start()
    local = pltpu.make_async_copy(blocks.at[pl.ds(place, 2)], slab.at[:, mine, :], own)
    local.start()

    def start(k, carry):
        remote(lax.rem(c + k, n_chan)).start()
        return carry

    lax.fori_loop(1, n_chan, start, 0)
    local.wait()

    def finish(k, carry):
        incoming(lax.rem(c + n_chan - k, n_chan)).wait_recv()
        return carry

    lax.fori_loop(1, n_chan, finish, 0)
    at_edge = jnp.logical_or(place == 0, place == count - 1)

    @pl.when(at_edge)
    def _():
        def take(source, carry):
            pltpu.make_async_remote_copy(
                src_ref=blocks.at[0],
                dst_ref=edge.at[pl.ds(pl.multiple_of(source * rows, rows), rows), :],
                send_sem=edge_send.at[0],
                recv_sem=edge_recv.at[source],
                device_id=(source, lax.rem(t + 1, n_tm)),
                device_id_type=MESH,
            ).wait_recv()
            return carry

        lax.fori_loop(0, n_chan, take, 0)

    left = lax.broadcasted_iota(jnp.int32, edge.shape, 1) < HALF

    @pl.when(place == 0)
    def _():
        slab[0] = jnp.where(left, edge[...], slab[0])

    @pl.when(place == count - 1)
    def _():
        slab[1] = jnp.where(left, slab[1], edge[...])

    def sent(k, carry):
        remote(lax.rem(c + k, n_chan)).wait_send()
        return carry

    lax.fori_loop(1, n_chan, sent, 0)
    for r in range(rep):
        rim(r, 1, r).wait_send()
        rim((count - 1) * rep + r, n_tm - 1, rep + r).wait_send()


def shrink(aa, ab, ba, bb, cut_one, cut_two):
    root_half = 1.0 / math.sqrt(2.0)
    re1 = (aa - bb) * root_half
    im1 = (ab + ba) * root_half
    re2 = (aa + bb) * root_half
    im2 = (ab - ba) * root_half
    f1 = jnp.maximum(1.0 - cut_one * lax.rsqrt(re1 * re1 + im1 * im1), 0.0) * root_half
    f2 = jnp.maximum(1.0 - cut_two * lax.rsqrt(re2 * re2 + im2 * im2), 0.0) * root_half
    re1, im1, re2, im2 = re1 * f1, im1 * f1, re2 * f2, im2 * f2
    return re1 + re2, im1 + im2, im1 - im2, re2 - re1


def cut_maps(cuts, level, shape, low_rows, low_cols):
    row_low = lax.broadcasted_iota(jnp.int32, shape, 0) < low_rows
    col_low = lax.broadcasted_iota(jnp.int32, shape, 1) < low_cols
    pick = []
    for k in range(2):
        lh, hl, hh = (cuts[level, 2 * o + k].astype(jnp.float32) / 32.0 for o in range(3))
        pick.append(jnp.where(row_low, lh, jnp.where(col_low, hl, hh)))
    return pick[0], pick[1], jnp.logical_and(row_low, col_low)


def denoise_kernel(
    cuts, slab, sources, c1, c1t, t1, t1c, c2, c2t, t2, t2t, c3, c3t, t3, t3t,
    picked, cleaned, coefs,
):
    trees = [(0, 0), (0, 1), (1, 0), (1, 1)]
    rows = slab.shape[1]
    cols = 2 * BLOCK
    x = split(jnp.concatenate([slab[0], slab[1]], 1))
    first = split(dot3(x, (t1[0], t1[1]), True))
    coefs[...] = dot3((c1[0], c1[1]), first)
    hr, hc = rows // 2, cols // 2
    lows = []
    for p, q in trees:
        band = split(coefs[p * rows : p * rows + hr, q * cols : q * cols + hc])
        timed = split(dot3(band, (t2[0, q], t2[1, q]), True))
        lows.append(dot3((c2[0, p], c2[1, p]), timed))
    deep = []
    for tree, (p, q) in enumerate(trees):
        timed = split(dot3(split(lows[tree]), (t3[0, q], t3[1, q]), True))
        deep.append(dot3((c3[0, p], c3[1, p]), timed))
    one, two, kept = cut_maps(cuts, 2, deep[0].shape, hr // 4, hc // 4)
    shrunk = shrink(*deep, one, two)
    deep = [jnp.where(kept, a, b) for a, b in zip(deep, shrunk)]
    one, two, kept = cut_maps(cuts, 1, lows[0].shape, hr // 2, hc // 2)
    shrunk = shrink(*lows, one, two)
    for orient, (row_high, col_high) in enumerate([(0, 1), (1, 0), (1, 1)]):
        spots = [
            (
                slice(p * rows + row_high * hr, p * rows + row_high * hr + hr),
                slice(q * cols + col_high * hc, q * cols + col_high * hc + hc),
            )
            for p, q in trees
        ]
        top = [
            cuts[0, 2 * orient + k].astype(jnp.float32) / 32.0 for k in range(2)
        ]
        done = shrink(*[coefs[a, b] for a, b in spots], top[0], top[1])
        for (a, b), cell in zip(spots, done):
            coefs[a, b] = cell
    for tree, (p, q) in enumerate(trees):
        timed = split(dot3(split(deep[tree]), (t3t[0, q], t3t[1, q]), True))
        inner = dot3((c3t[0, p], c3t[1, p]), timed)
        band = jnp.where(kept, inner, shrunk[tree])
        timed = split(dot3(split(band), (t2t[0, q], t2t[1, q]), True))
        coefs[p * rows : p * rows + hr, q * cols : q * cols + hc] = dot3(
            (c2t[0, p], c2t[1, p]), timed
        )
    timed = split(dot3(split(coefs[...]), (t1c[0], t1c[1])))
    result = (0.25 * dot3((c1t[0], c1t[1]), timed)).astype(jnp.bfloat16)
    cleaned[...] = result.astype(jnp.float32)
    one_hot = jnp.where(
        lax.broadcasted_iota(jnp.int32, (sources.shape[0], rows), 1) == sources[...], 1.0, 0.0
    ).astype(jnp.bfloat16)
    picked[...] = dot(one_hot, result, False).astype(jnp.bfloat16)


def spread_kernel(picked, cleaned, picks, receivers, send, recv, send2, recv2, own):
    n_chan, n_tm = lax.axis_size("chan"), lax.axis_size("tm")
    c, t = lax.axis_index("chan"), lax.axis_index("tm")
    per_window = N // BLOCK
    blocks = picks.shape[0] * per_window
    count = blocks // n_tm
    rep = n_chan // count
    share = cleaned.shape[0] // (n_chan * n_tm)
    greet_all()

    def spot(block):
        return block // per_window, pl.ds(
            pl.multiple_of(lax.rem(block, per_window) * BLOCK, BLOCK), BLOCK
        )

    def rows_of(dc, dt):
        return pl.ds(pl.multiple_of((dc * n_tm + dt) * share // 8 * 8, 8), 8)

    w, cols = spot(t * count + c // rep)
    first = pltpu.make_async_copy(picked, picks.at[w, :, cols], own.at[0])
    second = pltpu.make_async_copy(
        cleaned.at[rows_of(c, t), :], receivers.at[w, :, cols], own.at[1]
    )

    def pair(k):
        dc = lax.rem(c // rep + k // n_tm, count) * rep + lax.rem(c, rep)
        dt = lax.rem(t + lax.rem(k, n_tm), n_tm)
        block = t * count + c // rep
        return (
            pltpu.make_async_remote_copy(
                src_ref=picked,
                dst_ref=picks.at[w, :, cols],
                send_sem=send.at[k],
                recv_sem=recv.at[block],
                device_id=(dc, dt),
                device_id_type=MESH,
            ),
            pltpu.make_async_remote_copy(
                src_ref=cleaned.at[rows_of(dc, dt), :],
                dst_ref=receivers.at[w, :, cols],
                send_sem=send2.at[k],
                recv_sem=recv2.at[block],
                device_id=(dc, dt),
                device_id_type=MESH,
            ),
        )

    def start(k, carry):
        for copy in pair(k):
            copy.start()
        return carry

    lax.fori_loop(1, blocks, start, 0)
    first.start()
    second.start()
    first.wait()
    second.wait()

    def finish(k, carry):
        block = lax.rem(t * count + c // rep + k, blocks)
        bw, bcols = spot(block)
        away = (lax.rem(block, count) * rep, block // count)
        pltpu.make_async_remote_copy(
            src_ref=picked,
            dst_ref=picks.at[bw, :, bcols],
            send_sem=send.at[0],
            recv_sem=recv.at[block],
            device_id=away,
            device_id_type=MESH,
        ).wait_recv()
        pltpu.make_async_remote_copy(
            src_ref=cleaned.at[pl.ds(0, 8), :],
            dst_ref=receivers.at[bw, :, bcols],
            send_sem=send2.at[0],
            recv_sem=recv2.at[block],
            device_id=away,
            device_id_type=MESH,
        ).wait_recv()
        return carry

    lax.fori_loop(1, blocks, finish, 0)

    def sent(k, carry):
        for copy in pair(k):
            copy.wait_send()
        return carry

    lax.fori_loop(1, blocks, sent, 0)


def correlate_kernel(picks, receivers, table, out, white, heard, cross):
    windows, sources = picks.shape[0], picks.shape[1]

    def whiten(block):
        spectra = dot(block, table[...], False)
        scale = lax.rsqrt(jnp.mean(spectra * spectra, axis=1, keepdims=True) + 1e-05)
        return (spectra * scale).astype(jnp.bfloat16).astype(jnp.float32)

    joined = jnp.concatenate(
        [picks[...].reshape(windows * sources, N)]
        + [receivers[...].reshape(windows * 8, N).astype(jnp.bfloat16)],
        0,
    )
    spectra = whiten(joined)
    base = windows * sources
    for part in range(N // BLOCK):
        white[part] = spectra[:base, BLOCK * part : BLOCK * (part + 1)]
    for w in range(windows):
        heard[w] = spectra[base + 8 * w : base + 8 * w + 8]
    weight = jnp.where(lax.broadcasted_iota(jnp.int32, (1, BLOCK), 1) == 0, 1.0, 2.0)

    def body(g, carry):
        for chunk in range(BINS // BLOCK):
            lo = chunk * BLOCK
            hi = BINS + lo
            real = [None, None]
            imag = [None, None]
            for w in range(windows):
                rr = heard[w, :, lo : lo + BLOCK]
                ri = heard[w, :, hi : hi + BLOCK]
                for j in range(2):
                    spread = pl.ds(w * sources + 2 * g + j, 8, stride=0)
                    pr = white.at[chunk][spread, :]
                    pi = white.at[chunk + BINS // BLOCK][spread, :]
                    a = pr * rr + pi * ri
                    b = pi * rr - pr * ri
                    real[j] = a if real[j] is None else real[j] + a
                    imag[j] = b if imag[j] is None else imag[j] + b
            factor = weight if chunk == 0 else 2.0
            spot = pl.ds(pl.multiple_of(16 * g, 16), 16)
            cross[spot, lo : lo + BLOCK] = (jnp.concatenate(real, 0) * factor).astype(jnp.bfloat16)
            cross[spot, hi : hi + BLOCK] = (jnp.concatenate(imag, 0) * factor).astype(jnp.bfloat16)
        return carry

    lax.fori_loop(0, sources // 2, body, 0)
    scale = 1.0 / math.sqrt(windows * N)
    half = LAGS // 2
    lags = jnp.concatenate([table[N - half :, :], table[:half, :]], 0)
    out[...] = dot(cross[...], lags, True) * scale


def local(samples, thresholds, sources):
    n_chan, n_tm = lax.axis_size("chan"), lax.axis_size("tm")
    rows, width = samples.shape
    channels = rows * n_chan
    count = width // BLOCK
    rep = n_chan // count
    blocks = count * n_tm
    windows = n_tm * width // N
    picked_count = sources.shape[0]
    vmem = pl.BlockSpec(memory_space=pltpu.VMEM)
    smem = pl.BlockSpec(memory_space=pltpu.SMEM)
    dma = pltpu.SemaphoreType.DMA
    f32, bf16 = jnp.float32, jnp.bfloat16
    big = 60 * 1024 * 1024

    slab = pl.pallas_call(
        gather_kernel,
        out_shape=jax.ShapeDtypeStruct((2, channels, BLOCK), f32),
        in_specs=[vmem],
        out_specs=vmem,
        scratch_shapes=[
            pltpu.VMEM((count + 1, rows, BLOCK), f32),
            pltpu.VMEM((channels, BLOCK), f32),
            dma((n_chan,)),
            dma((n_chan,)),
            dma((2 * rep,)),
            dma((n_chan,)),
            dma,
        ],
        compiler_params=pltpu.CompilerParams(collective_id=0, has_side_effects=True),
        name="gather_slab",
    )(samples)

    def wide(matrix):
        return halves(matrix.reshape(-1, matrix.shape[-1]))

    def flipped(matrix):
        return np.swapaxes(matrix, -1, -2)

    def padded_low(matrix):
        return np.concatenate([matrix, np.zeros_like(matrix)], -1)

    chan = [bank_matrix(channels >> j) for j in range(3)]
    time = [bank_matrix(2 * BLOCK >> j) for j in range(3)]
    c1, t1 = wide(chan[0]), wide(time[0])
    c3, t3 = padded_low(chan[2]), padded_low(time[2])
    tables = [
        c1,
        np.ascontiguousarray(flipped(c1)),
        t1,
        np.ascontiguousarray(t1[:, :, HALF : HALF + BLOCK]),
        halves(chan[1]),
        halves(flipped(chan[1])),
        halves(time[1]),
        halves(flipped(time[1])),
        halves(c3),
        halves(flipped(c3)),
        halves(t3),
        halves(flipped(t3)),
    ]
    picked, cleaned = pl.pallas_call(
        denoise_kernel,
        out_shape=(
            jax.ShapeDtypeStruct((picked_count, BLOCK), bf16),
            jax.ShapeDtypeStruct((channels, BLOCK), f32),
        ),
        in_specs=[smem] + [vmem] * (2 + len(tables)),
        out_specs=(vmem, vmem),
        scratch_shapes=[pltpu.VMEM((2 * channels, 4 * BLOCK), f32)],
        compiler_params=pltpu.CompilerParams(vmem_limit_bytes=big),
        name="denoise",
    )(thresholds, slab, sources[:, None], *[jnp.asarray(a) for a in tables])

    picks, receivers = pl.pallas_call(
        spread_kernel,
        out_shape=(
            jax.ShapeDtypeStruct((windows, picked_count, N), bf16),
            jax.ShapeDtypeStruct((windows, 8, N), f32),
        ),
        in_specs=[vmem, vmem],
        out_specs=(vmem, vmem),
        scratch_shapes=[dma((blocks,)), dma((blocks,)), dma((blocks,)), dma((blocks,)), dma((2,))],
        compiler_params=pltpu.CompilerParams(collective_id=1, has_side_effects=True),
        name="spread",
    )(picked, cleaned)

    out = pl.pallas_call(
        correlate_kernel,
        out_shape=jax.ShapeDtypeStruct((picked_count * 8, LAGS), f32),
        in_specs=[vmem] * 3,
        out_specs=vmem,
        scratch_shapes=[
            pltpu.VMEM((N // BLOCK, windows * picked_count, BLOCK), f32),
            pltpu.VMEM((windows, 8, N), f32),
            pltpu.VMEM((picked_count * 8, N), bf16),
        ],
        compiler_params=pltpu.CompilerParams(vmem_limit_bytes=big),
        name="correlate",
    )(picks, receivers, jnp.asarray(dft_table()))
    out = out.reshape(picked_count, 8, LAGS)
    share = channels // (n_chan * n_tm)
    if share < 8:
        place = lax.axis_index("chan") * n_tm + lax.axis_index("tm")
        out = lax.dynamic_slice_in_dim(out, lax.rem(place * share, 8), share, 1)
    return out


def solution(mesh):
    return jax.shard_map(
        local,
        mesh=mesh,
        in_specs=(P("chan", "tm"), P(), P()),
        out_specs=P(None, ("chan", "tm"), None),
        check_vma=False,
    )
```

profile of v0, /device:TPU:13, one launch (start us, length us, event | category | flops | bytes accessed | tf_op | source)
XLA Modules:
  0.0 54.2 jit_solution(17600060791532716545)
XLA Ops:
  0.0 1.3 %copy.17.sources = s32[64,1]{1,0:T(8,128)} copy(s32[64,1]{0,1:T(1,128)} %bitcast.2) | data formatting | bytes 512 | tf_op jit(solution)/shard_map/broadcast_in_dim | solution.py:486
  1.3 14.6 %gather_slab.1.slab = f32[2,256,128]{2,1,0:T(8,128)} custom-call(f32[32,1024]{1,0:T(8,128)} %samples.1), custom_call_target="tpu_custom_call" | custom-call | tf_op jit(solution)/shard_map/gather_slab/pallas_call | solution.py:430
  16.0 9.0 %denoise.1 = (bf16[64,128]{1,0:T(8,128)(2,1)}, f32[256,128]{1,0:T(8,128)}) custom-call(s32[3,6]{1,0:T(4,128)} %cuts.1, f32[2,256,128]{2,1,0:T(8,128)} %gather_slab.1.slab, s32[64,1]{1,0:T(8,128)} %copy.17.sources, bf16[2,512,256]{2,1,0:T(8,128)(2,1)} %constant.16.clone.c1.t1, bf16[2,256,512]{2,1,0:T(8,128)(2,1)} %constant.17.clone.c1t, ...), custom_call_target="tpu_custom_call" | custom-call | tf_op jit(solution)/shard_map/denoise/pallas_call | solution.py:475
  24.9 23.2 %spread.1 = (bf16[4,64,1024]{2,1,0:T(8,128)(2,1)}, f32[4,8,1024]{2,1,0:T(8,128)}) custom-call(bf16[64,128]{1,0:T(8,128)(2,1)} %get-tuple-element.9.picked, f32[256,128]{1,0:T(8,128)} %get-tuple-element.10.cleaned), custom_call_target="tpu_custom_call" | custom-call | tf_op jit(solution)/shard_map/spread/pallas_call | solution.py:488
  48.2 6.0 %correlate.1 = f32[512,512]{1,0:T(8,128)} custom-call(bf16[4,64,1024]{2,1,0:T(8,128)(2,1)} %get-tuple-element.11.picks, f32[4,8,1024]{2,1,0:T(8,128)} %get-tuple-element.12.receivers, bf16[1024,1024]{1,0:T(8,128)(2,1)} %constant.23.clone.table), custom_call_target="tpu_custom_call" | custom-call | tf_op jit(solution)/shard_map/correlate/pallas_call | solution.py:501
where the time goes:
time: 54.4 us; the launch traced here: 54.2 us
  Pallas kernels  52.8 us (97%)
  local copies, waits for them, and re-layouts  1.35 us (2%)
    pallas_call x1, Pallas kernels, local(): pl.pallas_call(spread_kernel, out_shape=(jax.ShapeDtypeStruct((windows, p...  23.2 us
    pallas_call x1, Pallas kernels, local(): pl.pallas_call(gather_kernel, out_shape=jax.ShapeDtypeStruct((2, channels...  14.6 us
    pallas_call x1, Pallas kernels, local(): pl.pallas_call(denoise_kernel, out_shape=(jax.ShapeDtypeStruct((picked_co...  8.95 us
    pallas_call x1, Pallas kernels, local(): pl.pallas_call(correlate_kernel, out_shape=jax.ShapeDtypeStruct((picked_c...  6.01 us
    broadcast_in_dim x1, local copies, waits for them, and re-layouts, local(): sources[:, None]  1.35 us

commit v1 on v0

--- a/solution.py
+++ b/solution.py
@@ -1,3 +1,4 @@
+import functools
 import math
 
 import jax
@@ -92,25 +93,27 @@
     pl.semaphore_wait(barrier, n - 1)
 
 
-def gather_kernel(samples, slab, blocks, edge, send, recv, edge_send, edge_recv, own):
+def gather(samples, slab, blocks, edge, send, recv, edge_send, edge_recv, own):
     n_chan, n_tm = lax.axis_size("chan"), lax.axis_size("tm")
     c, t = lax.axis_index("chan"), lax.axis_index("tm")
     rows, width = samples.shape
     count = width // BLOCK
     rep = n_chan // count
     values = samples[...]
-    first = jnp.concatenate([values[:, width - HALF :], values[:, :HALF]], 1)
-    blocks[0] = first
-    blocks[count] = first
-    for j in range(1, count):
-        blocks[j] = values[:, BLOCK * j - HALF : BLOCK * j + HALF]
+    for j in range(count):
+        right, left = (BLOCK * (j + 1)) % width, (BLOCK * j - HALF) % width
+        blocks[2 * j] = values[:, BLOCK * j : BLOCK * (j + 1)]
+        blocks[2 * j + 1] = jnp.concatenate(
+            [values[:, right : right + HALF], values[:, left : left + HALF]], 1
+        )
+    blocks[2 * count] = jnp.concatenate([values[:, :HALF], values[:, width - HALF :]], 1)
     greet_all()
     mine = pl.ds(pl.multiple_of(c * rows, rows), rows)
     place = c // rep
 
     def remote(to):
         return pltpu.make_async_remote_copy(
-            src_ref=blocks.at[pl.ds(to // rep, 2)],
+            src_ref=blocks.at[pl.ds(to // rep * 2, 2)],
             dst_ref=slab.at[:, mine, :],
             send_sem=send.at[to],
             recv_sem=recv.at[c],
@@ -130,7 +133,7 @@
 
     def rim(to, shift, r):
         return pltpu.make_async_remote_copy(
-            src_ref=blocks.at[0],
+            src_ref=blocks.at[2 * count],
             dst_ref=edge.at[mine, :],
             send_sem=edge_send.at[r],
             recv_sem=edge_recv.at[c],
@@ -141,7 +144,7 @@
     for r in range(rep):
         rim(r, 1, r).start()
         rim((count - 1) * rep + r, n_tm - 1, rep + r).start()
-    local = pltpu.make_async_copy(blocks.at[pl.ds(place, 2)], slab.at[:, mine, :], own)
+    local = pltpu.make_async_copy(blocks.at[pl.ds(place * 2, 2)], slab.at[:, mine, :], own)
     local.start()
 
     def start(k, carry):
@@ -162,7 +165,7 @@
     def _():
         def take(source, carry):
             pltpu.make_async_remote_copy(
-                src_ref=blocks.at[0],
+                src_ref=blocks.at[2 * count],
                 dst_ref=edge.at[pl.ds(pl.multiple_of(source * rows, rows), rows), :],
                 send_sem=edge_send.at[0],
                 recv_sem=edge_recv.at[source],
@@ -177,11 +180,11 @@
 
     @pl.when(place == 0)
     def _():
-        slab[0] = jnp.where(left, edge[...], slab[0])
+        slab[1] = jnp.where(left, slab[1], edge[...])
 
     @pl.when(place == count - 1)
     def _():
-        slab[1] = jnp.where(left, slab[1], edge[...])
+        slab[1] = jnp.where(left, edge[...], slab[1])
 
     def sent(k, carry):
         remote(lax.rem(c + k, n_chan)).wait_send()
@@ -215,10 +218,8 @@
     return pick[0], pick[1], jnp.logical_and(row_low, col_low)
 
 
-def denoise_kernel(
-    cuts, slab, sources, c1, c1t, t1, t1c, c2, c2t, t2, t2t, c3, c3t, t3, t3t,
-    picked, cleaned, coefs,
-):
+def denoise(cuts, slab, sources, tables, picked, cleaned, coefs):
+    c1, c1t, t1, c2, c2t, t2, t2t, c3, c3t, t3, t3t = tables
     trees = [(0, 0), (0, 1), (1, 0), (1, 1)]
     rows = slab.shape[1]
     cols = 2 * BLOCK
@@ -262,116 +263,164 @@
         coefs[p * rows : p * rows + hr, q * cols : q * cols + hc] = dot3(
             (c2t[0, p], c2t[1, p]), timed
         )
-    timed = split(dot3(split(coefs[...]), (t1c[0], t1c[1])))
+    timed = split(dot3(split(coefs[...]), (t1[0, :, :BLOCK], t1[1, :, :BLOCK])))
     result = (0.25 * dot3((c1t[0], c1t[1]), timed)).astype(jnp.bfloat16)
-    cleaned[...] = result.astype(jnp.float32)
+    cleaned[...] = result.astype(jnp.float32).reshape(rows // 8, 8, BLOCK).astype(jnp.bfloat16)
     one_hot = jnp.where(
-        lax.broadcasted_iota(jnp.int32, (sources.shape[0], rows), 1) == sources[...], 1.0, 0.0
-    ).astype(jnp.bfloat16)
-    picked[...] = dot(one_hot, result, False).astype(jnp.bfloat16)
-
-
-def spread_kernel(picked, cleaned, picks, receivers, send, recv, send2, recv2, own):
+        lax.broadcasted_iota(jnp.int32, (rows, sources.shape[1]), 0) == sources[...], 1.0, 0.0
+    )
+    chosen = jnp.transpose(one_hot).astype(jnp.bfloat16)
+    picked[...] = dot(chosen, result, False).astype(jnp.bfloat16)
+
+
+def spread(picks, cleaned, receivers, near, far, across, recv, send, land, own):
     n_chan, n_tm = lax.axis_size("chan"), lax.axis_size("tm")
     c, t = lax.axis_index("chan"), lax.axis_index("tm")
-    per_window = N // BLOCK
-    blocks = picks.shape[0] * per_window
+    blocks = picks.shape[0]
     count = blocks // n_tm
     rep = n_chan // count
-    share = cleaned.shape[0] // (n_chan * n_tm)
-    greet_all()
-
-    def spot(block):
-        return block // per_window, pl.ds(
-            pl.multiple_of(lax.rem(block, per_window) * BLOCK, BLOCK), BLOCK
-        )
+    pairs = n_tm // 2
+    share = cleaned.shape[0] * 8 // (n_chan * n_tm)
+    place, copy_index, core = c // rep, lax.rem(c, rep), lax.rem(t, 2)
+    mine = t * count + place
+
+    def move(block, sem, chan, tm):
+        return pltpu.make_async_remote_copy(
+            src_ref=picks.at[block],
+            dst_ref=picks.at[block],
+            send_sem=sem,
+            recv_sem=recv.at[block],
+            device_id=(chan, tm),
+            device_id_type=MESH,
+        )
+
+    def group(k):
+        return move(mine, near.at[k], lax.rem(place + k, count) * rep + copy_index, t)
+
+    def along(u, k):
+        block = t * count + lax.rem(place + count - k, count)
+        to = lax.rem(t // 2 + u, pairs) * 2 + core
+        return move(block, far.at[u * count + k], c, to)
+
+    def beside(u, k):
+        other = lax.rem(t // 2 + pairs - u, pairs) * 2 + core
+        block = other * count + lax.rem(place + count - k, count)
+        return move(block, across.at[u * count + k], c, t + 1 - 2 * core)
 
     def rows_of(dc, dt):
-        return pl.ds(pl.multiple_of((dc * n_tm + dt) * share // 8 * 8, 8), 8)
-
-    w, cols = spot(t * count + c // rep)
-    first = pltpu.make_async_copy(picked, picks.at[w, :, cols], own.at[0])
-    second = pltpu.make_async_copy(
-        cleaned.at[rows_of(c, t), :], receivers.at[w, :, cols], own.at[1]
-    )
-
-    def pair(k):
-        dc = lax.rem(c // rep + k // n_tm, count) * rep + lax.rem(c, rep)
+        return (dc * n_tm + dt) * share // 8
+
+    def personal(k):
+        dc = lax.rem(place + k // n_tm, count) * rep + copy_index
         dt = lax.rem(t + lax.rem(k, n_tm), n_tm)
-        block = t * count + c // rep
-        return (
-            pltpu.make_async_remote_copy(
-                src_ref=picked,
-                dst_ref=picks.at[w, :, cols],
-                send_sem=send.at[k],
-                recv_sem=recv.at[block],
-                device_id=(dc, dt),
-                device_id_type=MESH,
-            ),
-            pltpu.make_async_remote_copy(
-                src_ref=cleaned.at[rows_of(dc, dt), :],
-                dst_ref=receivers.at[w, :, cols],
-                send_sem=send2.at[k],
-                recv_sem=recv2.at[block],
-                device_id=(dc, dt),
-                device_id_type=MESH,
-            ),
-        )
-
-    def start(k, carry):
-        for copy in pair(k):
-            copy.start()
-        return carry
-
-    lax.fori_loop(1, blocks, start, 0)
-    first.start()
-    second.start()
-    first.wait()
-    second.wait()
-
-    def finish(k, carry):
-        block = lax.rem(t * count + c // rep + k, blocks)
-        bw, bcols = spot(block)
-        away = (lax.rem(block, count) * rep, block // count)
+        return pltpu.make_async_remote_copy(
+            src_ref=cleaned.at[rows_of(dc, dt)],
+            dst_ref=receivers.at[mine],
+            send_sem=send.at[k],
+            recv_sem=land.at[mine],
+            device_id=(dc, dt),
+            device_id_type=MESH,
+        )
+
+    def each(low, high, act):
+        def body(k, carry):
+            act(k)
+            return carry
+
+        lax.fori_loop(low, high, body, 0)
+
+    def await_block(block):
+        move(block, near.at[0], c, t + 1 - 2 * core).wait_recv()
+
+    def relay(k):
+        @pl.when(k > 0)
+        def _():
+            await_block(t * count + lax.rem(place + count - k, count))
+
+        for u in range(1, pairs):
+            along(u, k).start()
+        beside(0, k).start()
+
+    each(1, count, lambda k: group(k).start())
+    local = pltpu.make_async_copy(cleaned.at[rows_of(c, t)], receivers.at[mine], own)
+    local.start()
+    relay(0)
+    each(1, blocks, lambda k: personal(k).start())
+    each(1, count, relay)
+    for u in range(1, pairs):
+
+        def cross_over(k, u=u):
+            other = lax.rem(t // 2 + pairs - u, pairs) * 2 + core
+            await_block(other * count + lax.rem(place + count - k, count))
+            beside(u, k).start()
+
+        each(0, count, cross_over)
+    for u in range(pairs):
+
+        def last(k, u=u):
+            other = lax.rem(t // 2 + pairs - u, pairs) * 2 + 1 - core
+            await_block(other * count + lax.rem(place + count - k, count))
+
+        each(0, count, last)
+
+    def landed(k):
+        block = lax.rem(mine + k, blocks)
         pltpu.make_async_remote_copy(
-            src_ref=picked,
-            dst_ref=picks.at[bw, :, bcols],
+            src_ref=cleaned.at[0],
+            dst_ref=receivers.at[block],
             send_sem=send.at[0],
-            recv_sem=recv.at[block],
-            device_id=away,
+            recv_sem=land.at[block],
+            device_id=(c, t + 1 - 2 * core),
             device_id_type=MESH,
         ).wait_recv()
-        pltpu.make_async_remote_copy(
-            src_ref=cleaned.at[pl.ds(0, 8), :],
-            dst_ref=receivers.at[bw, :, bcols],
-            send_sem=send2.at[0],
-            recv_sem=recv2.at[block],
-            device_id=away,
-            device_id_type=MESH,
-        ).wait_recv()
-        return carry
-
-    lax.fori_loop(1, blocks, finish, 0)
-
-    def sent(k, carry):
-        for copy in pair(k):
-            copy.wait_send()
-        return carry
-
-    lax.fori_loop(1, blocks, sent, 0)
+
+    local.wait()
+    each(1, blocks, landed)
+    each(1, count, lambda k: group(k).wait_send())
+    each(1, blocks, lambda k: personal(k).wait_send())
+    for u in range(pairs):
+        each(0, count, lambda k, u=u: beside(u, k).wait_send())
+        if u:
+            each(0, count, lambda k, u=u: along(u, k).wait_send())
+
+
+def clean_kernel(n_tables, same, cuts, samples, sources, *refs):
+    stored, refs = refs[:n_tables], refs[n_tables:]
+    picks, receivers = refs[:2]
+    held, refs = refs[2 : 2 + n_tables], refs[2 + n_tables :]
+    slab, blocks, edge, coefs, cleaned, loads = refs[:6]
+    gather_sems, spread_sems = refs[6:11], refs[11:]
+    copies = [pltpu.make_async_copy(a, b, loads.at[i]) for i, (a, b) in enumerate(zip(stored, held))]
+    for copy in copies:
+        copy.start()
+    gather(samples, slab, blocks, edge, *gather_sems)
+    for copy in copies:
+        copy.wait()
+    tables = [held[1], *held] if same else list(held)
+    n_tm = lax.axis_size("tm")
+    count = picks.shape[0] // n_tm
+    rep = lax.axis_size("chan") // count
+    mine = lax.axis_index("tm") * count + lax.axis_index("chan") // rep
+    denoise(cuts, slab, sources, tables, picks.at[mine], cleaned, coefs)
+    spread(picks, cleaned, receivers, *spread_sems)
 
 
 def correlate_kernel(picks, receivers, table, out, white, heard, cross):
-    windows, sources = picks.shape[0], picks.shape[1]
+    per_window = N // BLOCK
+    windows, sources = picks.shape[0] // per_window, picks.shape[1]
+
+    def window(ref, w):
+        return jnp.concatenate([ref[w * per_window + j] for j in range(per_window)], 1)
 
     def whiten(block):
         spectra = dot(block, table[...], False)
         scale = lax.rsqrt(jnp.mean(spectra * spectra, axis=1, keepdims=True) + 1e-05)
         return (spectra * scale).astype(jnp.bfloat16).astype(jnp.float32)
 
+    heard_rows = [window(receivers, w).astype(jnp.float32) for w in range(windows)]
     joined = jnp.concatenate(
-        [picks[...].reshape(windows * sources, N)]
-        + [receivers[...].reshape(windows * 8, N).astype(jnp.bfloat16)],
+        [window(picks, w) for w in range(windows)]
+        + [jnp.concatenate(heard_rows, 0).astype(jnp.bfloat16)],
         0,
     )
     spectra = whiten(joined)
@@ -427,24 +476,6 @@
     f32, bf16 = jnp.float32, jnp.bfloat16
     big = 60 * 1024 * 1024
 
-    slab = pl.pallas_call(
-        gather_kernel,
-        out_shape=jax.ShapeDtypeStruct((2, channels, BLOCK), f32),
-        in_specs=[vmem],
-        out_specs=vmem,
-        scratch_shapes=[
-            pltpu.VMEM((count + 1, rows, BLOCK), f32),
-            pltpu.VMEM((channels, BLOCK), f32),
-            dma((n_chan,)),
-            dma((n_chan,)),
-            dma((2 * rep,)),
-            dma((n_chan,)),
-            dma,
-        ],
-        compiler_params=pltpu.CompilerParams(collective_id=0, has_side_effects=True),
-        name="gather_slab",
-    )(samples)
-
     def wide(matrix):
         return halves(matrix.reshape(-1, matrix.shape[-1]))
 
@@ -458,11 +489,10 @@
     time = [bank_matrix(2 * BLOCK >> j) for j in range(3)]
     c1, t1 = wide(chan[0]), wide(time[0])
     c3, t3 = padded_low(chan[2]), padded_low(time[2])
-    tables = [
-        c1,
+    same = channels == 2 * BLOCK
+    tables = ([] if same else [c1]) + [
         np.ascontiguousarray(flipped(c1)),
         t1,
-        np.ascontiguousarray(t1[:, :, HALF : HALF + BLOCK]),
         halves(chan[1]),
         halves(flipped(chan[1])),
         halves(time[1]),
@@ -472,31 +502,41 @@
         halves(t3),
         halves(flipped(t3)),
     ]
-    picked, cleaned = pl.pallas_call(
-        denoise_kernel,
+    far_count = blocks // 2
+    picks, receivers = pl.pallas_call(
+        functools.partial(clean_kernel, len(tables), same),
         out_shape=(
-            jax.ShapeDtypeStruct((picked_count, BLOCK), bf16),
-            jax.ShapeDtypeStruct((channels, BLOCK), f32),
+            jax.ShapeDtypeStruct((blocks, picked_count, BLOCK), bf16),
+            jax.ShapeDtypeStruct((blocks, 8, BLOCK), bf16),
         ),
-        in_specs=[smem] + [vmem] * (2 + len(tables)),
+        in_specs=[smem, vmem, vmem] + [pl.BlockSpec(memory_space=pl.ANY)] * len(tables),
         out_specs=(vmem, vmem),
-        scratch_shapes=[pltpu.VMEM((2 * channels, 4 * BLOCK), f32)],
-        compiler_params=pltpu.CompilerParams(vmem_limit_bytes=big),
-        name="denoise",
-    )(thresholds, slab, sources[:, None], *[jnp.asarray(a) for a in tables])
-
-    picks, receivers = pl.pallas_call(
-        spread_kernel,
-        out_shape=(
-            jax.ShapeDtypeStruct((windows, picked_count, N), bf16),
-            jax.ShapeDtypeStruct((windows, 8, N), f32),
+        scratch_shapes=[pltpu.VMEM(a.shape, bf16) for a in tables]
+        + [
+            pltpu.VMEM((2, channels, BLOCK), f32),
+            pltpu.VMEM((2 * count + 1, rows, BLOCK), f32),
+            pltpu.VMEM((channels, BLOCK), f32),
+            pltpu.VMEM((2 * channels, 4 * BLOCK), f32),
+            pltpu.VMEM((channels // 8, 8, BLOCK), bf16),
+            dma((len(tables),)),
+            dma((n_chan,)),
+            dma((n_chan,)),
+            dma((2 * rep,)),
+            dma((n_chan,)),
+            dma,
+            dma((count,)),
+            dma((far_count,)),
+            dma((far_count,)),
+            dma((blocks,)),
+            dma((blocks,)),
+            dma((blocks,)),
+            dma,
+        ],
+        compiler_params=pltpu.CompilerParams(
+            collective_id=0, has_side_effects=True, vmem_limit_bytes=big
         ),
-        in_specs=[vmem, vmem],
-        out_specs=(vmem, vmem),
-        scratch_shapes=[dma((blocks,)), dma((blocks,)), dma((blocks,)), dma((blocks,)), dma((2,))],
-        compiler_params=pltpu.CompilerParams(collective_id=1, has_side_effects=True),
-        name="spread",
-    )(picked, cleaned)
+        name="clean",
+    )(thresholds, samples, sources[None, :], *[jnp.asarray(a) for a in tables])
 
     out = pl.pallas_call(
         correlate_kernel,

time: 54.4 us -> 41 us (0.75)
  the two profiles are of different devices: /device:TPU:13 before, /device:TPU:1 now
where the time goes in v1:
time: 41 us; the launch traced here: 40.8 us
  Pallas kernels  40.8 us (100%)
    pallas_call x1, Pallas kernels, local(): pl.pallas_call(functools.partial(clean_kernel, len(tables), same), out_sh...  34.8 us
    pallas_call x1, Pallas kernels, local(): pl.pallas_call(correlate_kernel, out_shape=jax.ShapeDtypeStruct((picked_c...  5.99 us

profile of v1, /device:TPU:1, one launch (start us, length us, event | category | flops | bytes accessed | tf_op | source)
XLA Modules:
  0.0 40.8 jit_solution(5995369160203106837)
XLA Ops:
  0.0 34.8 %clean.1 = (bf16[32,64,128]{2,1,0:T(8,128)(2,1)}, bf16[32,8,128]{2,1,0:T(8,128)(2,1)}) custom-call(s32[3,6]{1,0:T(4,128)} %cuts.1, f32[32,1024]{1,0:T(8,128)} %samples.1, s32[1,64]{1,0:T(1,128)} %bitcast.2, bf16[2,256,512]{2,1,0:T(8,128)(2,1)} %constant.14.clone.refs_0_, bf16[2,512,256]{2,1,0:T(8,128)(2,1)} %constant.15.clone.refs_1_, ...), custom_call_target="tpu_custom_call" | custom-call | tf_op jit(solution)/shard_map/clean/pallas_call | solution.py:506
  34.8 6.0 %correlate.1 = f32[512,512]{1,0:T(8,128)} custom-call(bf16[32,64,128]{2,1,0:T(8,128)(2,1)} %get-tuple-element.7.picks, bf16[32,8,128]{2,1,0:T(8,128)(2,1)} %get-tuple-element.8.receivers, bf16[1024,1024]{1,0:T(8,128)(2,1)} %constant.20.clone.table), custom_call_target="tpu_custom_call" | custom-call | tf_op jit(solution)/shard_map/correlate/pallas_call | solution.py:541

commit v2 on v1

--- a/solution.py
+++ b/solution.py
@@ -218,6 +218,38 @@
     return pick[0], pick[1], jnp.logical_and(row_low, col_low)
 
 
+def packed(matrix):
+    hi, lo = halves(matrix)
+    return np.concatenate(
+        [np.concatenate([hi, hi], -1), np.concatenate([lo, np.zeros_like(lo)], -1)], -2
+    )
+
+
+def by_rows(x, weight):
+    y = dot(jnp.concatenate(split(x), 1), weight, True)
+    half = weight.shape[0] // 2
+    return y[:, :half] + y[:, half:]
+
+
+def by_cols(weight, x):
+    y = dot(weight, jnp.concatenate(split(x), 0), False)
+    half = weight.shape[0] // 2
+    return y[:half] + y[half:]
+
+
+def both_ways(bands, chan_weight, time_weight):
+    rows, cols = bands[0].shape
+    timed = []
+    for q in range(2):
+        timed.append(by_rows(jnp.concatenate([bands[q], bands[2 + q]], 0), time_weight[q]))
+    out = []
+    for p in range(2):
+        part = slice(p * rows, (p + 1) * rows)
+        y = by_cols(chan_weight[p], jnp.concatenate([timed[0][part], timed[1][part]], 1))
+        out += [y[:, :cols], y[:, cols:]]
+    return out
+
+
 def denoise(cuts, slab, sources, tables, picked, cleaned, coefs):
     c1, c1t, t1, c2, c2t, t2, t2t, c3, c3t, t3, t3t = tables
     trees = [(0, 0), (0, 1), (1, 0), (1, 1)]
@@ -227,20 +259,21 @@
     first = split(dot3(x, (t1[0], t1[1]), True))
     coefs[...] = dot3((c1[0], c1[1]), first)
     hr, hc = rows // 2, cols // 2
-    lows = []
-    for p, q in trees:
-        band = split(coefs[p * rows : p * rows + hr, q * cols : q * cols + hc])
-        timed = split(dot3(band, (t2[0, q], t2[1, q]), True))
-        lows.append(dot3((c2[0, p], c2[1, p]), timed))
-    deep = []
-    for tree, (p, q) in enumerate(trees):
-        timed = split(dot3(split(lows[tree]), (t3[0, q], t3[1, q]), True))
-        deep.append(dot3((c3[0, p], c3[1, p]), timed))
+    corners = [
+        (slice(p * rows, p * rows + hr), slice(q * cols, q * cols + hc)) for p, q in trees
+    ]
+    lows = both_ways([coefs[a, b] for a, b in corners], c2, t2)
+    deep = both_ways(lows, c3, t3)
+    live = hr // 2
+    deep = [band[:live] for band in deep]
     one, two, kept = cut_maps(cuts, 2, deep[0].shape, hr // 4, hc // 4)
     shrunk = shrink(*deep, one, two)
     deep = [jnp.where(kept, a, b) for a, b in zip(deep, shrunk)]
+    rest = jnp.zeros((hr - live, hc), jnp.float32)
+    inner = both_ways([jnp.concatenate([band, rest], 0) for band in deep], c3t, t3t)
     one, two, kept = cut_maps(cuts, 1, lows[0].shape, hr // 2, hc // 2)
     shrunk = shrink(*lows, one, two)
+    outer = both_ways([jnp.where(kept, a, b) for a, b in zip(inner, shrunk)], c2t, t2t)
     for orient, (row_high, col_high) in enumerate([(0, 1), (1, 0), (1, 1)]):
         spots = [
             (
@@ -255,16 +288,15 @@
         done = shrink(*[coefs[a, b] for a, b in spots], top[0], top[1])
         for (a, b), cell in zip(spots, done):
             coefs[a, b] = cell
-    for tree, (p, q) in enumerate(trees):
-        timed = split(dot3(split(deep[tree]), (t3t[0, q], t3t[1, q]), True))
-        inner = dot3((c3t[0, p], c3t[1, p]), timed)
-        band = jnp.where(kept, inner, shrunk[tree])
-        timed = split(dot3(split(band), (t2t[0, q], t2t[1, q]), True))
-        coefs[p * rows : p * rows + hr, q * cols : q * cols + hc] = dot3(
-            (c2t[0, p], c2t[1, p]), timed
-        )
-    timed = split(dot3(split(coefs[...]), (t1[0, :, :BLOCK], t1[1, :, :BLOCK])))
-    result = (0.25 * dot3((c1t[0], c1t[1]), timed)).astype(jnp.bfloat16)
+    for (a, b), band in zip(corners, outer):
+        coefs[a, b] = band
+    hi, lo = split(coefs[...])
+    t_hi, t_lo = t1[0, :, :BLOCK], t1[1, :, :BLOCK]
+    y = dot(hi, jnp.concatenate([t_hi, t_lo], 1), False)
+    timed = jnp.concatenate(split(y[:, :BLOCK] + y[:, BLOCK:] + dot(lo, t_hi, False)), 1)
+    y = dot(c1t[0], timed, False)
+    whole = y[:, :BLOCK] + y[:, BLOCK:] + dot(c1t[1], timed[:, :BLOCK], False)
+    result = (0.25 * whole).astype(jnp.bfloat16)
     cleaned[...] = result.astype(jnp.float32).reshape(rows // 8, 8, BLOCK).astype(jnp.bfloat16)
     one_hot = jnp.where(
         lax.broadcasted_iota(jnp.int32, (rows, sources.shape[1]), 0) == sources[...], 1.0, 0.0
@@ -396,7 +428,9 @@
     gather(samples, slab, blocks, edge, *gather_sems)
     for copy in copies:
         copy.wait()
-    tables = [held[1], *held] if same else list(held)
+    c1t, t1, c2, c2t, c3, c3t = held[:6]
+    extra = [t1, c2, c2t, c3, c3t] if same else held[6:]
+    tables = [extra[0], c1t, t1, extra[1], extra[2], c2, c2t, extra[3], extra[4], c3, c3t]
     n_tm = lax.axis_size("tm")
     count = picks.shape[0] // n_tm
     rep = lax.axis_size("chan") // count
@@ -482,26 +516,21 @@
     def flipped(matrix):
         return np.swapaxes(matrix, -1, -2)
 
-    def padded_low(matrix):
-        return np.concatenate([matrix, np.zeros_like(matrix)], -1)
-
-    chan = [bank_matrix(channels >> j) for j in range(3)]
-    time = [bank_matrix(2 * BLOCK >> j) for j in range(3)]
-    c1, t1 = wide(chan[0]), wide(time[0])
-    c3, t3 = padded_low(chan[2]), padded_low(time[2])
+    def cornered(matrix):
+        size = matrix.shape[-1]
+        return np.pad(matrix, ((0, 0), (0, size), (0, size)))
+
+    def pack_pair(length):
+        second, third = bank_matrix(length // 2), cornered(bank_matrix(length // 4))
+        return [packed(m) for m in (second, flipped(second), third, flipped(third))]
+
     same = channels == 2 * BLOCK
-    tables = ([] if same else [c1]) + [
-        np.ascontiguousarray(flipped(c1)),
-        t1,
-        halves(chan[1]),
-        halves(flipped(chan[1])),
-        halves(time[1]),
-        halves(flipped(time[1])),
-        halves(c3),
-        halves(flipped(c3)),
-        halves(t3),
-        halves(flipped(t3)),
-    ]
+    c1, t1 = wide(bank_matrix(channels)), wide(bank_matrix(2 * BLOCK))
+    chan, time = pack_pair(channels), pack_pair(2 * BLOCK)
+    tables = [np.ascontiguousarray(flipped(c1)), t1, *time]
+    if not same:
+        tables += [c1, *chan]
+
     far_count = blocks // 2
     picks, receivers = pl.pallas_call(
         functools.partial(clean_kernel, len(tables), same),

time: 41 us -> 37.6 us (0.917)
  Pallas kernels: 40.8 us -> 37.4 us
    pallas_call x1, Pallas kernels: 34.8 us -> 31.4 us  [local(): pl.pallas_call(functools.partial(clean_kernel, len(tables), same), out_sh...]
where the time goes in v2:
time: 37.6 us; the launch traced here: 37.4 us
  Pallas kernels  37.4 us (99%)
    pallas_call x1, Pallas kernels, local(): pl.pallas_call(functools.partial(clean_kernel, len(tables), same), out_sh...  31.4 us
    pallas_call x1, Pallas kernels, local(): pl.pallas_call(correlate_kernel, out_shape=jax.ShapeDtypeStruct((picked_c...  5.98 us

profile of v2, /device:TPU:1, one launch (start us, length us, event | category | flops | bytes accessed | tf_op | source)
XLA Modules:
  0.0 37.4 jit_solution(1752251133154427490)
XLA Ops:
  0.0 31.4 %clean.1 = (bf16[32,64,128]{2,1,0:T(8,128)(2,1)}, bf16[32,8,128]{2,1,0:T(8,128)(2,1)}) custom-call(s32[3,6]{1,0:T(4,128)} %cuts.1, f32[32,1024]{1,0:T(8,128)} %samples.1, s32[1,64]{1,0:T(1,128)} %bitcast.2, bf16[2,256,512]{2,1,0:T(8,128)(2,1)} %constant.14.clone.refs_0_, bf16[2,512,256]{2,1,0:T(8,128)(2,1)} %constant.15.clone.refs_1_, ...), custom_call_target="tpu_custom_call" | custom-call | tf_op jit(solution)/shard_map/clean/pallas_call | solution.py:535
  31.4 6.0 %correlate.1 = f32[512,512]{1,0:T(8,128)} custom-call(bf16[32,64,128]{2,1,0:T(8,128)(2,1)} %get-tuple-element.7.picks, bf16[32,8,128]{2,1,0:T(8,128)(2,1)} %get-tuple-element.8.receivers, bf16[1024,1024]{1,0:T(8,128)(2,1)} %constant.20.clone.table), custom_call_target="tpu_custom_call" | custom-call | tf_op jit(solution)/shard_map/correlate/pallas_call | solution.py:570

commit v3 on v2

--- a/solution.py
+++ b/solution.py
@@ -93,7 +93,9 @@
     pl.semaphore_wait(barrier, n - 1)
 
 
-def gather(samples, slab, blocks, edge, send, recv, edge_send, edge_recv, own):
+def gather(
+    samples, slab, rim_slab, blocks, rims, edge, send, recv, edge_send, edge_recv
+):
     n_chan, n_tm = lax.axis_size("chan"), lax.axis_size("tm")
     c, t = lax.axis_index("chan"), lax.axis_index("tm")
     rows, width = samples.shape
@@ -102,38 +104,46 @@
     values = samples[...]
     for j in range(count):
         right, left = (BLOCK * (j + 1)) % width, (BLOCK * j - HALF) % width
-        blocks[2 * j] = values[:, BLOCK * j : BLOCK * (j + 1)]
-        blocks[2 * j + 1] = jnp.concatenate(
+        blocks[j] = values[:, BLOCK * j : BLOCK * (j + 1)]
+        rims[j] = jnp.concatenate(
             [values[:, right : right + HALF], values[:, left : left + HALF]], 1
-        )
-    blocks[2 * count] = jnp.concatenate([values[:, :HALF], values[:, width - HALF :]], 1)
+        ).astype(jnp.bfloat16)
+    rims[count] = jnp.concatenate([values[:, :HALF], values[:, width - HALF :]], 1).astype(
+        jnp.bfloat16
+    )
     greet_all()
     mine = pl.ds(pl.multiple_of(c * rows, rows), rows)
     place = c // rep
 
+    def pair(to, rows_at, landing):
+        return (
+            pltpu.make_async_remote_copy(
+                src_ref=blocks.at[to // rep],
+                dst_ref=slab.at[rows_at, :],
+                send_sem=send.at[to],
+                recv_sem=recv.at[landing],
+                device_id=(to, t),
+                device_id_type=MESH,
+            ),
+            pltpu.make_async_remote_copy(
+                src_ref=rims.at[to // rep],
+                dst_ref=rim_slab.at[rows_at, :],
+                send_sem=send.at[n_chan + to],
+                recv_sem=recv.at[n_chan + landing],
+                device_id=(to, t),
+                device_id_type=MESH,
+            ),
+        )
+
     def remote(to):
-        return pltpu.make_async_remote_copy(
-            src_ref=blocks.at[pl.ds(to // rep * 2, 2)],
-            dst_ref=slab.at[:, mine, :],
-            send_sem=send.at[to],
-            recv_sem=recv.at[c],
-            device_id=(to, t),
-            device_id_type=MESH,
-        )
+        return pair(to, mine, c)
 
     def incoming(source):
-        return pltpu.make_async_remote_copy(
-            src_ref=blocks.at[pl.ds(0, 2)],
-            dst_ref=slab.at[:, pl.ds(pl.multiple_of(source * rows, rows), rows), :],
-            send_sem=send.at[source],
-            recv_sem=recv.at[source],
-            device_id=(source, t),
-            device_id_type=MESH,
-        )
+        return pair(source, pl.ds(pl.multiple_of(source * rows, rows), rows), source)
 
     def rim(to, shift, r):
         return pltpu.make_async_remote_copy(
-            src_ref=blocks.at[2 * count],
+            src_ref=rims.at[count],
             dst_ref=edge.at[mine, :],
             send_sem=edge_send.at[r],
             recv_sem=edge_recv.at[c],
@@ -144,18 +154,19 @@
     for r in range(rep):
         rim(r, 1, r).start()
         rim((count - 1) * rep + r, n_tm - 1, rep + r).start()
-    local = pltpu.make_async_copy(blocks.at[pl.ds(place * 2, 2)], slab.at[:, mine, :], own)
-    local.start()
+    slab[mine, :] = blocks[place]
+    rim_slab[mine, :] = rims[place]
 
     def start(k, carry):
-        remote(lax.rem(c + k, n_chan)).start()
+        for copy in remote(lax.rem(c + k, n_chan)):
+            copy.start()
         return carry
 
     lax.fori_loop(1, n_chan, start, 0)
-    local.wait()
 
     def finish(k, carry):
-        incoming(lax.rem(c + n_chan - k, n_chan)).wait_recv()
+        for copy in incoming(lax.rem(c + n_chan - k, n_chan)):
+            copy.wait_recv()
         return carry
 
     lax.fori_loop(1, n_chan, finish, 0)
@@ -165,7 +176,7 @@
     def _():
         def take(source, carry):
             pltpu.make_async_remote_copy(
-                src_ref=blocks.at[2 * count],
+                src_ref=rims.at[count],
                 dst_ref=edge.at[pl.ds(pl.multiple_of(source * rows, rows), rows), :],
                 send_sem=edge_send.at[0],
                 recv_sem=edge_recv.at[source],
@@ -180,14 +191,15 @@
 
     @pl.when(place == 0)
     def _():
-        slab[1] = jnp.where(left, slab[1], edge[...])
+        rim_slab[...] = jnp.where(left, rim_slab[...], edge[...])
 
     @pl.when(place == count - 1)
     def _():
-        slab[1] = jnp.where(left, edge[...], slab[1])
+        rim_slab[...] = jnp.where(left, edge[...], rim_slab[...])
 
     def sent(k, carry):
-        remote(lax.rem(c + k, n_chan)).wait_send()
+        for copy in remote(lax.rem(c + k, n_chan)):
+            copy.wait_send()
         return carry
 
     lax.fori_loop(1, n_chan, sent, 0)
@@ -250,12 +262,14 @@
     return out
 
 
-def denoise(cuts, slab, sources, tables, picked, cleaned, coefs):
+def denoise(cuts, slab, rim_slab, sources, tables, picked, cleaned, coefs):
     c1, c1t, t1, c2, c2t, t2, t2t, c3, c3t, t3, t3t = tables
     trees = [(0, 0), (0, 1), (1, 0), (1, 1)]
-    rows = slab.shape[1]
+    rows = slab.shape[0]
     cols = 2 * BLOCK
-    x = split(jnp.concatenate([slab[0], slab[1]], 1))
+    hi, lo = split(slab[...])
+    rim = rim_slab[...]
+    x = jnp.concatenate([hi, rim], 1), jnp.concatenate([lo, jnp.zeros_like(rim)], 1)
     first = split(dot3(x, (t1[0], t1[1]), True))
     coefs[...] = dot3((c1[0], c1[1]), first)
     hr, hc = rows // 2, cols // 2
@@ -416,30 +430,32 @@
             each(0, count, lambda k, u=u: along(u, k).wait_send())
 
 
-def clean_kernel(n_tables, same, cuts, samples, sources, *refs):
+def whole_kernel(n_tables, same, cuts, samples, sources, *refs):
     stored, refs = refs[:n_tables], refs[n_tables:]
-    picks, receivers = refs[:2]
-    held, refs = refs[2 : 2 + n_tables], refs[2 + n_tables :]
-    slab, blocks, edge, coefs, cleaned, loads = refs[:6]
-    gather_sems, spread_sems = refs[6:11], refs[11:]
+    out, picks, receivers, white, heard, cross = refs[:6]
+    held, refs = refs[6 : 6 + n_tables], refs[6 + n_tables :]
+    slab, rim_slab, blocks, rims, edge, coefs, cleaned, loads = refs[:8]
+    gather_sems, spread_sems = refs[8:12], refs[12:]
     copies = [pltpu.make_async_copy(a, b, loads.at[i]) for i, (a, b) in enumerate(zip(stored, held))]
     for copy in copies:
         copy.start()
-    gather(samples, slab, blocks, edge, *gather_sems)
-    for copy in copies:
+    gather(samples, slab, rim_slab, blocks, rims, edge, *gather_sems)
+    for copy in copies[:-1]:
         copy.wait()
     c1t, t1, c2, c2t, c3, c3t = held[:6]
-    extra = [t1, c2, c2t, c3, c3t] if same else held[6:]
+    extra = [t1, c2, c2t, c3, c3t] if same else held[6:-1]
     tables = [extra[0], c1t, t1, extra[1], extra[2], c2, c2t, extra[3], extra[4], c3, c3t]
     n_tm = lax.axis_size("tm")
     count = picks.shape[0] // n_tm
     rep = lax.axis_size("chan") // count
     mine = lax.axis_index("tm") * count + lax.axis_index("chan") // rep
-    denoise(cuts, slab, sources, tables, picks.at[mine], cleaned, coefs)
+    denoise(cuts, slab, rim_slab, sources, tables, picks.at[mine], cleaned, coefs)
     spread(picks, cleaned, receivers, *spread_sems)
-
-
-def correlate_kernel(picks, receivers, table, out, white, heard, cross):
+    copies[-1].wait()
+    correlate(picks, receivers, held[-1], out, white, heard, cross)
+
+
+def correlate(picks, receivers, table, out, white, heard, cross):
     per_window = N // BLOCK
     windows, sources = picks.shape[0] // per_window, picks.shape[1]
 
@@ -530,29 +546,35 @@
     tables = [np.ascontiguousarray(flipped(c1)), t1, *time]
     if not same:
         tables += [c1, *chan]
+    tables.append(dft_table())
 
     far_count = blocks // 2
-    picks, receivers = pl.pallas_call(
-        functools.partial(clean_kernel, len(tables), same),
-        out_shape=(
-            jax.ShapeDtypeStruct((blocks, picked_count, BLOCK), bf16),
-            jax.ShapeDtypeStruct((blocks, 8, BLOCK), bf16),
-        ),
+    out = pl.pallas_call(
+        functools.partial(whole_kernel, len(tables), same),
+        out_shape=jax.ShapeDtypeStruct((picked_count * 8, LAGS), f32),
         in_specs=[smem, vmem, vmem] + [pl.BlockSpec(memory_space=pl.ANY)] * len(tables),
-        out_specs=(vmem, vmem),
-        scratch_shapes=[pltpu.VMEM(a.shape, bf16) for a in tables]
+        out_specs=vmem,
+        scratch_shapes=[
+            pltpu.VMEM((blocks, picked_count, BLOCK), bf16),
+            pltpu.VMEM((blocks, 8, BLOCK), bf16),
+            pltpu.VMEM((N // BLOCK, windows * picked_count, BLOCK), f32),
+            pltpu.VMEM((windows, 8, N), f32),
+            pltpu.VMEM((picked_count * 8, N), bf16),
+        ]
+        + [pltpu.VMEM(a.shape, bf16) for a in tables]
         + [
-            pltpu.VMEM((2, channels, BLOCK), f32),
-            pltpu.VMEM((2 * count + 1, rows, BLOCK), f32),
             pltpu.VMEM((channels, BLOCK), f32),
+            pltpu.VMEM((channels, BLOCK), bf16),
+            pltpu.VMEM((count, rows, BLOCK), f32),
+            pltpu.VMEM((count + 1, rows, BLOCK), bf16),
+            pltpu.VMEM((channels, BLOCK), bf16),
             pltpu.VMEM((2 * channels, 4 * BLOCK), f32),
             pltpu.VMEM((channels // 8, 8, BLOCK), bf16),
             dma((len(tables),)),
-            dma((n_chan,)),
-            dma((n_chan,)),
+            dma((2 * n_chan,)),
+            dma((2 * n_chan,)),
             dma((2 * rep,)),
             dma((n_chan,)),
-            dma,
             dma((count,)),
             dma((far_count,)),
             dma((far_count,)),
@@ -564,22 +586,9 @@
         compiler_params=pltpu.CompilerParams(
             collective_id=0, has_side_effects=True, vmem_limit_bytes=big
         ),
-        name="clean",
+        name="whole",
     )(thresholds, samples, sources[None, :], *[jnp.asarray(a) for a in tables])
 
-    out = pl.pallas_call(
-        correlate_kernel,
-        out_shape=jax.ShapeDtypeStruct((picked_count * 8, LAGS), f32),
-        in_specs=[vmem] * 3,
-        out_specs=vmem,
-        scratch_shapes=[
-            pltpu.VMEM((N // BLOCK, windows * picked_count, BLOCK), f32),
-            pltpu.VMEM((windows, 8, N), f32),
-            pltpu.VMEM((picked_count * 8, N), bf16),
-        ],
-        compiler_params=pltpu.CompilerParams(vmem_limit_bytes=big),
-        name="correlate",
-    )(picks, receivers, jnp.asarray(dft_table()))
     out = out.reshape(picked_count, 8, LAGS)
     share = channels // (n_chan * n_tm)
     if share < 8:

time: 37.6 us -> 35.6 us (0.947)
  Pallas kernels: 37.4 us -> 33.1 us
  local copies, waits for them, and re-layouts: 0 us -> 2.26 us
    pallas_call x2 -> x1, Pallas kernels: 37.4 us -> 33.1 us  [local(): pl.pallas_call(functools.partial(whole_kernel, len(tables), same), out_sh...]
    unnamed x0 -> x1, local copies, waits for them, and re-layouts: none -> 2.26 us
where the time goes in v3:
time: 35.6 us; the launch traced here: 35.4 us
  Pallas kernels  33.1 us (93%)
  local copies, waits for them, and re-layouts  2.26 us (6%)
    pallas_call x1, Pallas kernels, local(): pl.pallas_call(functools.partial(whole_kernel, len(tables), same), out_sh...  33.1 us
    unnamed x1, local copies, waits for them, and re-layouts  2.26 us

profile of v3, /device:TPU:1, one launch (start us, length us, event | category | flops | bytes accessed | tf_op | source)
XLA Modules:
  0.0 35.4 jit_solution(1348943612607089206)
XLA Ops:
  0.0 33.1 %whole.1 = f32[512,512]{1,0:T(8,128)} custom-call(s32[3,6]{1,0:T(4,128)} %cuts.1, f32[32,1024]{1,0:T(8,128)} %samples.1, s32[1,64]{1,0:T(1,128)} %bitcast.3, bf16[2,256,512]{2,1,0:T(8,128)(2,1)} %constant.14.clone.refs_0_, bf16[2,512,256]{2,1,0:T(8,128)(2,1)} %constant.15.clone.refs_1_, bf16[2,256,256]{2,1,0:T(8,128)(2,1)} %constant.16.clone.refs_2_, ...), custom_call_target="tpu_custom_call" | custom-call | tf_op jit(solution)/shard_map/whole/pallas_call | solution.py:552
  33.1 2.3 %copy.12 = f32[64,8,512]{2,1,0:T(8,128)} copy(f32[64,8,512]{2,1,0:T(8,128)} %bitcast.2) | data formatting | bytes 2097152

commit v4 on v3

--- a/solution.py
+++ b/solution.py
@@ -344,9 +344,9 @@
         return move(mine, near.at[k], lax.rem(place + k, count) * rep + copy_index, t)
 
     def along(u, k):
-        block = t * count + lax.rem(place + count - k, count)
         to = lax.rem(t // 2 + u, pairs) * 2 + core
-        return move(block, far.at[u * count + k], c, to)
+        chan = lax.rem(place + k, count) * rep + copy_index
+        return move(mine, far.at[u * count + k], chan, to)
 
     def beside(u, k):
         other = lax.rem(t // 2 + pairs - u, pairs) * 2 + core
@@ -383,11 +383,11 @@
         def _():
             await_block(t * count + lax.rem(place + count - k, count))
 
-        for u in range(1, pairs):
-            along(u, k).start()
         beside(0, k).start()
 
     each(1, count, lambda k: group(k).start())
+    for u in range(1, pairs):
+        each(0, count, lambda k, u=u: along(u, k).start())
     local = pltpu.make_async_copy(cleaned.at[rows_of(c, t)], receivers.at[mine], own)
     local.start()
     relay(0)

time: 35.6 us -> 34 us (0.955)
  Pallas kernels: 33.1 us -> 31.6 us
    pallas_call x1, Pallas kernels: 33.1 us -> 31.6 us  [local(): pl.pallas_call(functools.partial(whole_kernel, len(tables), same), out_sh...]
where the time goes in v4:
time: 34 us; the launch traced here: 33.9 us
  Pallas kernels  31.6 us (93%)
  local copies, waits for them, and re-layouts  2.26 us (7%)
    pallas_call x1, Pallas kernels, local(): pl.pallas_call(functools.partial(whole_kernel, len(tables), same), out_sh...  31.6 us
    unnamed x1, local copies, waits for them, and re-layouts  2.26 us

profile of v4, /device:TPU:1, one launch (start us, length us, event | category | flops | bytes accessed | tf_op | source)
XLA Modules:
  0.0 33.9 jit_solution(8991105340992557895)
XLA Ops:
  0.0 31.6 %whole.1 = f32[512,512]{1,0:T(8,128)} custom-call(s32[3,6]{1,0:T(4,128)} %cuts.1, f32[32,1024]{1,0:T(8,128)} %samples.1, s32[1,64]{1,0:T(1,128)} %bitcast.3, bf16[2,256,512]{2,1,0:T(8,128)(2,1)} %constant.14.clone.refs_0_, bf16[2,512,256]{2,1,0:T(8,128)(2,1)} %constant.15.clone.refs_1_, bf16[2,256,256]{2,1,0:T(8,128)(2,1)} %constant.16.clone.refs_2_, ...), custom_call_target="tpu_custom_call" | custom-call | tf_op jit(solution)/shard_map/whole/pallas_call | solution.py:552
  31.6 2.3 %copy.12 = f32[64,8,512]{2,1,0:T(8,128)} copy(f32[64,8,512]{2,1,0:T(8,128)} %bitcast.2) | data formatting | bytes 2097152
